TPU v7x, 512 devices: a whole 4x4x16 slice. The times are simulated.
512 devices in a mesh: wide: 64 (over z, x_lo, core), narrow: 8 (over y, x_hi).
Axes of the slice: x: 4 (x_hi: 2, x_lo: 2; x = x_hi * 2 + x_lo), y: 4, z: 16, core: 2. Of those that a mesh axis runs over, the one named last changes fastest.
Arguments:
- features: bfloat16 [512, 64, 8, 192], P('wide', 'narrow'), may hold values from -6 to 6
- weight: bfloat16 [5184, 192], replicated, may hold values from -0.078125 to 0.078125
- voxel_mask: int32 [512, 64, 8], P('wide', 'narrow'), may hold values 0 or 1
- cotangent: bfloat16 [512, 64, 8, 192], P('wide', 'narrow'), may hold values from -16 to 16
Outputs:
- activation: bfloat16 [512, 64, 8, 192], P('wide', 'narrow')
- grad_input: bfloat16 [512, 64, 8, 192], P('wide', 'narrow')
- grad_weight: float32 [192, 5184], P('wide')
All inputs are finite; a program needn't handle non-finite values. No bound on the sum of `voxel_mask` on one device may be relied on, other than what follows from the above.
Results may differ from a plain program's by a relative error of at most 0.0049.
Values may be sent and summed in bfloat16 or wider, within the bound.
A program may use at most 64 MiB of HBM per device.

v0:
```python
import jax
import jax.numpy as jnp
from jax import lax
from jax.sharding import PartitionSpec as P


def padded_2(cells, sides, width):
    for axis, dim in sides:
        count = lax.axis_size(axis)
        ends = count - 1
        head = lax.slice_in_dim(cells, 0, width, axis=dim)
        tail = lax.slice_in_dim(cells, cells.shape[dim] - width, cells.shape[dim], axis=dim)
        cells = jnp.concatenate(
            [
                lax.ppermute(tail, axis, [(i, (i + 1) % count) for i in range(ends)]),
                cells,
                lax.ppermute(head, axis, [((i + 1) % count, i) for i in range(ends)]),
            ],
            axis=dim,
        )
    return cells


def gather_taps(padded, width_x, width_y, depth_z, channels, flip):
    pieces = []
    for shift_x in range(3):
        for shift_y in range(3):
            for shift_z in range(3):
                start_x = 2 - shift_x if flip else shift_x
                start_y = 2 - shift_y if flip else shift_y
                start_z = 2 - shift_z if flip else shift_z
                piece = padded[
                    start_x : start_x + width_x,
                    start_y : start_y + width_y,
                    start_z : start_z + depth_z,
                    :,
                ]
                pieces.append(piece.reshape(-1, channels))
    return jnp.concatenate(pieces, axis=1)


def local(features, weight, voxel_mask, cotangent):
    width_x, width_y, depth_z, channels = features.shape
    masked = features * voxel_mask.astype(jnp.bfloat16)[..., None]
    padded = padded_2(masked, (("wide", 0), ("narrow", 1)), 1)
    padded = jnp.pad(padded, ((0, 0), (0, 0), (1, 1), (0, 0)))
    columns = gather_taps(padded, width_x, width_y, depth_z, channels, False)
    pre = jnp.dot(columns, weight, preferred_element_type=jnp.float32)
    live = voxel_mask.reshape(-1, 1).astype(jnp.float32)
    sig = jax.nn.sigmoid(pre)
    activation = (
        (pre * sig * live).astype(jnp.bfloat16).reshape(width_x, width_y, depth_z, channels)
    )
    slope = sig * (1.0 + pre * (1.0 - sig))
    grad_pre = (cotangent.reshape(-1, channels).astype(jnp.float32) * live * slope).astype(
        jnp.bfloat16
    )
    taps = weight.reshape(27, channels, channels)
    grid = grad_pre.reshape(width_x, width_y, depth_z, channels)
    grad_pad = padded_2(grid, (("wide", 0), ("narrow", 1)), 1)
    grad_pad = jnp.pad(grad_pad, ((0, 0), (0, 0), (1, 1), (0, 0)))
    grad_columns = gather_taps(grad_pad, width_x, width_y, depth_z, channels, True)
    flipped = jnp.transpose(taps, (0, 2, 1)).reshape(27 * channels, channels)
    grad_field = jnp.dot(grad_columns, flipped, preferred_element_type=jnp.float32)
    grad_input = (
        (grad_field * live).astype(jnp.bfloat16).reshape(width_x, width_y, depth_z, channels)
    )
    scale = 1.0 / jnp.sqrt(
        jnp.float32(width_x * width_y * depth_z * lax.axis_size("wide") * lax.axis_size("narrow"))
    )
    share = lax.psum_scatter(
        lax.dot_general(
            grad_pre, columns, (((0,), (0,)), ((), ())), preferred_element_type=jnp.float32
        ),
        "wide",
        scatter_dimension=0,
        tiled=True,
    )
    summed = lax.psum(share, "narrow")
    grad_weight = summed * scale
    return (activation, grad_input, grad_weight)


def solution(mesh):
    return jax.shard_map(
        local,
        mesh=mesh,
        in_specs=(
            P("wide", "narrow", None, None),
            P(),
            P("wide", "narrow", None),
            P("wide", "narrow", None, None),
        ),
        out_specs=(
            P("wide", "narrow", None, None),
            P("wide", "narrow", None, None),
            P("wide", None),
        ),
        check_vma=False,
    )
```

profile of v0, /device:TPU:8, one launch (start us, length us, event | category | flops | bytes accessed | tf_op | source)
XLA Modules:
  0.0 576.8 jit_solution(6194891221397248752)
XLA Ops:
  8.1 1.1 broadcast_multiply_fusion
  9.2 1.7 collective-permute-start
  10.9 1.3 collective-permute-start.1
  12.2 1.0 bitcast_convert_fusion
  14.2 3.8 copy.77
  18.1 3.4 copy.78
  21.5 1.3 dynamic-slice
  23.5 4.9 collective-permute-start.2
  28.4 3.3 collective-permute-start.3
  32.6 3.2 collective-permute-done.3
  36.3 2.0 fusion.8
  38.4 1.2 fusion.11
  39.6 10.0 %concatenate.56 = bf16[512,5184]{1,0:T(8,128)(2,1)} concatenate(bf16[512,192]{1,0:T(8,128)(2,1)} %bitcast.96, bf16[512,192]{1,0:T(8,128)(2,1)} %bitcast.100, bf16[512,192]{1,0:T(8,128)(2,1)} %bitcast.95, bf16[512,192]{1,0:T(8,128)(2,1)} %bitcast.94, bf16[512,192]{1,0:T(8,128)(2,1)} %bitcast.122, bf16[512,192]{1,0:T(8,128)(2,1)} %bitcast.93, bf16[512,192]{1,0:T(8,128)(2,1)} %bitcast.92, ...), dimensions={1} | concatenate | bytes 10616832 | tf_op jit(solution)/shard_map/concatenate | solution.py:39
  49.6 4.6 multiply_convert_fusion
  54.5 1.3 collective-permute-start.5
  55.8 3.2 collective-permute-start.4
  59.1 5.7 fusion.16
  65.8 4.6 collective-permute-start.6
  70.5 3.8 collective-permute-start.7
  75.3 2.6 collective-permute-done.7
  83.4 1.7 fusion.7
  85.2 1.7 copy.76
  86.9 1.8 copy.74
  88.7 1.7 copy.73
  90.4 1.8 copy.71
  92.2 1.8 copy.70
  93.9 1.8 copy.68
  105.3 1.1 constant_dynamic-update-slice_fusion.26
  119.1 1.3 fusion.1
  121.3 405.2 %all-reduce.5.cloned.1.call-done = f32[192,5184]{1,0:T(8,128)} async-done(((f32[192,5184]{1,0:T(8,128)}), f32[192,5184]{1,0:T(8,128)}) %all-reduce.5.cloned.1.call-update) | async-done | bytes 3981328
  526.5 1.0 constant_dynamic-slice_fusion
  527.5 41.8 %psum.7 = f32[3,5184]{1,0:T(4,128)S(1)} all-reduce(f32[3,5184]{1,0:T(4,128)S(1)} %constant_dynamic-slice_fusion), channel_id=1, replica_groups=mesh['wide'=64,'narrow'=8] {'narrow'}, use_global_device_ids=true, to_apply=%region_1.2 | all-reduce | flops 15552 | bytes 124416 | tf_op jit(solution)/shard_map/psum | solution.py:79
  (101 shorter events, 34.9 us)
Async XLA Ops:
  7.2 519.3 %all-reduce.5.cloned.1.call-start = ((), (), s32[]{:S(2)}) async-start(), calls=%async_computation | async-start | bytes 8060928
  9.2 14.3 %collective-permute-start = (bf16[1,8,8,192]{3,2,1,0:T(8,128)(2,1)S(1)}, bf16[1,8,8,192]{3,2,1,0:T(8,128)(2,1)S(1)}, u32[]{:S(2)}, u32[]{:S(2)}) collective-permute-start(bf16[1,8,8,192]{3,2,1,0:T(8,128)(2,1)S(1)} %get-tuple-element.68), channel_id=1, source_target_pairs={{0,8},{8,16},{16,24},{24,32},{32,40},{40,48},{48,56},{56,64},{64,7... | collective-permute-start | bytes 73736 | tf_op jit(solution)/shard_map/ppermute | solution.py:15
  10.9 12.5 %collective-permute-start.1 = (bf16[1,8,8,192]{3,2,1,0:T(8,128)(2,1)S(1)}, bf16[1,8,8,192]{3,2,1,0:T(8,128)(2,1)S(1)}, u32[]{:S(2)}, u32[]{:S(2)}) collective-permute-start(bf16[1,8,8,192]{3,2,1,0:T(8,128)(2,1)S(1)} %get-tuple-element.69), channel_id=1, source_target_pairs={{8,0},{16,8},{24,16},{32,24},{40,32},{48,40},{56,48},{64,56},{72,6... | collective-permute-start | bytes 73736 | tf_op jit(solution)/shard_map/ppermute | solution.py:17
  23.5 9.2 %collective-permute-start.2 = (bf16[10,1,8,192]{3,2,1,0:T(8,128)(2,1)S(1)}, bf16[10,1,8,192]{3,2,1,0:T(8,128)(2,1)S(1)}, u32[]{:S(2)}, u32[]{:S(2)}) collective-permute-start(bf16[10,1,8,192]{3,2,1,0:T(8,128)(2,1)S(1)} %get-tuple-element.62), channel_id=1, source_target_pairs={{0,1},{1,2},{2,3},{3,4},{4,5},{5,6},{6,7},{8,9},{9,10},{10,11},{11... | collective-permute-start | bytes 92168 | tf_op jit(solution)/shard_map/ppermute | solution.py:15
  28.4 7.4 %collective-permute-start.3 = (bf16[10,1,8,192]{3,2,1,0:T(8,128)(2,1)S(1)}, bf16[10,1,8,192]{3,2,1,0:T(8,128)(2,1)S(1)}, u32[]{:S(2)}, u32[]{:S(2)}) collective-permute-start(bf16[10,1,8,192]{3,2,1,0:T(8,128)(2,1)S(1)} %get-tuple-element.63), channel_id=1, source_target_pairs={{1,0},{2,1},{3,2},{4,3},{5,4},{6,5},{7,6},{9,8},{10,9},{11,10},{12... | collective-permute-start | bytes 92168 | tf_op jit(solution)/shard_map/ppermute | solution.py:17
  39.6 10.0 %copy-start.1 = (bf16[5184,192]{0,1:T(8,128)(2,1)S(1)}, bf16[5184,192]{0,1:T(8,128)(2,1)}, u32[]{:S(2)}) copy-start(bf16[5184,192]{0,1:T(8,128)(2,1)} %param.5) | copy-start | bytes 5971972
  54.5 11.3 %collective-permute-start.5 = (bf16[1,8,8,192]{3,2,1,0:T(8,128)(2,1)S(1)}, bf16[1,8,8,192]{3,2,1,0:T(8,128)(2,1)S(1)}, u32[]{:S(2)}, u32[]{:S(2)}) collective-permute-start(bf16[1,8,8,192]{3,2,1,0:T(8,128)(2,1)S(1)} %bitcast.134), channel_id=1, source_target_pairs={{8,0},{16,8},{24,16},{32,24},{40,32},{48,40},{56,48},{64,56},{72,6... | collective-permute-start | bytes 73736 | tf_op jit(solution)/shard_map/ppermute | solution.py:17
  55.8 10.0 %collective-permute-start.4 = (bf16[1,8,8,192]{3,2,1,0:T(8,128)(2,1)S(1)}, bf16[1,8,8,192]{3,2,1,0:T(8,128)(2,1)S(1)}, u32[]{:S(2)}, u32[]{:S(2)}) collective-permute-start(bf16[1,8,8,192]{3,2,1,0:T(8,128)(2,1)S(1)} %bitcast.133), channel_id=1, source_target_pairs={{0,8},{8,16},{16,24},{24,32},{32,40},{40,48},{48,56},{56,64},{64,7... | collective-permute-start | bytes 73736 | tf_op jit(solution)/shard_map/ppermute | solution.py:15
  65.8 9.5 %collective-permute-start.6 = (bf16[10,1,8,192]{3,2,1,0:T(8,128)(2,1)S(1)}, bf16[10,1,8,192]{3,2,1,0:T(8,128)(2,1)S(1)}, u32[]{:S(2)}, u32[]{:S(2)}) collective-permute-start(bf16[10,1,8,192]{3,2,1,0:T(8,128)(2,1)S(1)} %get-tuple-element.58), channel_id=1, source_target_pairs={{0,1},{1,2},{2,3},{3,4},{4,5},{5,6},{6,7},{8,9},{9,10},{10,11},{11... | collective-permute-start | bytes 92168 | tf_op jit(solution)/shard_map/ppermute | solution.py:15
  70.5 7.4 %collective-permute-start.7 = (bf16[10,1,8,192]{3,2,1,0:T(8,128)(2,1)S(1)}, bf16[10,1,8,192]{3,2,1,0:T(8,128)(2,1)S(1)}, u32[]{:S(2)}, u32[]{:S(2)}) collective-permute-start(bf16[10,1,8,192]{3,2,1,0:T(8,128)(2,1)S(1)} %get-tuple-element.59), channel_id=1, source_target_pairs={{1,0},{2,1},{3,2},{4,3},{5,4},{6,5},{7,6},{9,8},{10,9},{11,10},{12... | collective-permute-start | bytes 92168 | tf_op jit(solution)/shard_map/ppermute | solution.py:17
  96.5 12.8 %copy-start.6 = (bf16[512,192]{0,1:T(8,128)(2,1)S(1)}, bf16[512,192]{0,1:T(8,128)(2,1)}, u32[]{:S(2)}) copy-start(bf16[512,192]{0,1:T(8,128)(2,1)} %copy.55) | copy-start | bytes 589828
  98.1 17.1 %copy-start.3 = (bf16[512,192]{0,1:T(8,128)(2,1)S(1)}, bf16[512,192]{0,1:T(8,128)(2,1)}, u32[]{:S(2)}) copy-start(bf16[512,192]{0,1:T(8,128)(2,1)} %copy.66) | copy-start | bytes 589828
  99.7 17.4 %copy-start.4 = (bf16[512,192]{0,1:T(8,128)(2,1)S(1)}, bf16[512,192]{0,1:T(8,128)(2,1)}, u32[]{:S(2)}) copy-start(bf16[512,192]{0,1:T(8,128)(2,1)} %copy.69) | copy-start | bytes 589828
  100.5 10.7 %copy-start.9 = (bf16[512,192]{0,1:T(8,128)(2,1)S(1)}, bf16[512,192]{0,1:T(8,128)(2,1)}, u32[]{:S(2)}) copy-start(bf16[512,192]{0,1:T(8,128)(2,1)} %copy.58) | copy-start | bytes 589828
  101.3 11.8 %copy-start.10 = (bf16[512,192]{0,1:T(8,128)(2,1)S(1)}, bf16[512,192]{0,1:T(8,128)(2,1)}, u32[]{:S(2)}) copy-start(bf16[512,192]{0,1:T(8,128)(2,1)} %copy.61) | copy-start | bytes 589828
  102.1 13.0 %copy-start.11 = (bf16[512,192]{0,1:T(8,128)(2,1)S(1)}, bf16[512,192]{0,1:T(8,128)(2,1)}, u32[]{:S(2)}) copy-start(bf16[512,192]{0,1:T(8,128)(2,1)} %copy.65) | copy-start | bytes 589828
  102.9 12.2 %copy-start.12 = (bf16[512,192]{0,1:T(8,128)(2,1)S(1)}, bf16[512,192]{0,1:T(8,128)(2,1)}, u32[]{:S(2)}) copy-start(bf16[512,192]{0,1:T(8,128)(2,1)} %copy.64) | copy-start | bytes 589828
  102.9 16.1 %copy-start.8 = (bf16[512,192]{0,1:T(8,128)(2,1)S(1)}, bf16[512,192]{0,1:T(8,128)(2,1)}, u32[]{:S(2)}) copy-start(bf16[512,192]{0,1:T(8,128)(2,1)} %copy.73) | copy-start | bytes 589828
  102.9 16.1 %copy-start.7 = (bf16[512,192]{0,1:T(8,128)(2,1)S(1)}, bf16[512,192]{0,1:T(8,128)(2,1)}, u32[]{:S(2)}) copy-start(bf16[512,192]{0,1:T(8,128)(2,1)} %copy.74) | copy-start | bytes 589828
  103.7 15.4 %copy-start.2 = (bf16[512,192]{0,1:T(8,128)(2,1)S(1)}, bf16[512,192]{0,1:T(8,128)(2,1)}, u32[]{:S(2)}) copy-start(bf16[512,192]{0,1:T(8,128)(2,1)} %copy.75) | copy-start | bytes 589828
  104.5 14.6 %copy-start.5 = (bf16[512,192]{0,1:T(8,128)(2,1)S(1)}, bf16[512,192]{0,1:T(8,128)(2,1)}, u32[]{:S(2)}) copy-start(bf16[512,192]{0,1:T(8,128)(2,1)} %copy.76) | copy-start | bytes 589828
  105.3 13.8 %copy-start = (bf16[27,192,192]{2,1,0:T(8,128)(2,1)S(1)}, bf16[27,192,192]{2,1,0:T(8,128)(2,1)}, u32[]{:S(2)}) copy-start(bf16[27,192,192]{2,1,0:T(8,128)(2,1)} %copy.78) | copy-start | bytes 5971972
Sparse Core Ops, SparseCore 0:
  65.1 461.3 all-reduce.4
where the time goes:
time: 579 us; the launch traced here: 577 us
  waiting for transfers between devices  411 us (71%)
  local copies, waits for them, and re-layouts  67.1 us (12%)
  blocking collectives  41.8 us (7%)
  starting transfers between devices  24.2 us (4%)
  between operations  15.2 us (3%)
  matrix products  11.7 us (2%)
    unnamed x2, waiting for transfers between devices  405 us
    psum x1, blocking collectives, local(): summed = lax.psum(share, 'narrow')  41.8 us
    reshape x26, local copies, waits for them, and re-layouts, gather_taps(): pieces.append(piece.reshape(-1, channels))  25.8 us
    unnamed x55, local copies, waits for them, and re-layouts  19.7 us
    ppermute x4, starting transfers between devices, padded_2(): lax.ppermute(tail, axis, [(i, (i + 1) % count) for i in range(ends)])  14.5 us
  transfers between devices with their start and end apart: 9, of which 3 were waited for; matrix products, arithmetic and copies ran while one was open for 11% of the time, Pallas kernels for 0%

commit v1 on v0

v1 whole, which is shorter than its diff:
```python
import jax
import jax.numpy as jnp
from jax import lax
from jax.experimental import pallas as pl
from jax.experimental.pallas import tpu as pltpu
from jax.sharding import PartitionSpec as P

C = 192
BF = jnp.bfloat16
F32 = jnp.float32
MESH = pl.DeviceIdType.MESH
WIDE, NARROW = 64, 8


def iota(shape, dim):
    return lax.broadcasted_iota(jnp.int32, shape, dim)


def build_shifts(src, even, odd, w, n):
    def body(x, carry):
        v = src[x].astype(F32)
        yy = iota((10, 8, C), 0)
        zz = iota((10, 8, C), 1)
        x_ok = jnp.logical_and(
            jnp.logical_or(x > 0, w > 0), jnp.logical_or(x < 9, w < WIDE - 1)
        )
        lo = jnp.where(n > 0, 0, 1)
        hi = jnp.where(n < NARROW - 1, 9, 8)
        lo = jnp.where(x_ok, lo, 100)
        v = jnp.where((yy >= lo) & (yy <= hi), v, 0.0)
        for c in range(3):
            if c == 0:
                s = jnp.where(zz == 0, 0.0, pltpu.roll(v, 1, 1))
            elif c == 1:
                s = v
            else:
                s = jnp.where(zz == 7, 0.0, pltpu.roll(v, 7, 1))
            s = s.reshape(80, C)
            even[c, x] = s.astype(BF)
            odd[c, x] = s[8:72].astype(BF)
        return carry

    lax.fori_loop(0, 10, body, 0)


def tap_rows(even, odd, a, b, c):
    if b == 1:
        v = odd[c, a : a + 8]
    else:
        v = even[c, a : a + 8, 8 * b : 8 * b + 64, :]
    return v.reshape(512, C)


def kernel(
    feat_hbm, w_hbm, mask_ref, cot_hbm,
    act_ref, gin_ref, gw_ref,
    wv, cot, halo, ghalo, even, odd, cols, pre, live, gp2, gpt,
    own, sb, rb, s1b, a1, b1, a1b, b1b, tb, zb, fin,
    ra, rby, ra2, rb2, rz, ag,
    lsem, hsend, hrecv, gsend, grecv, csend, crecv,
    asend, arecv, bsend, brecv, a2send, a2recv, b2send, b2recv,
    zsend, zrecv, gsnd, grcv,
):
    w = lax.axis_index("wide")
    n = lax.axis_index("narrow")
    core = w % 2
    xl = (w // 2) % 2
    z = w // 4
    y = n // 2
    xh = n % 2
    x = xh * 2 + xl

    def dev(z_, x_, c_, y_):
        return {"wide": (z_ * 2 + x_ % 2) * 2 + c_, "narrow": y_ * 2 + x_ // 2}

    near = []
    for dw, dn in ((1, 0), (-1, 0), (0, 1), (0, -1), (1, 1), (1, -1), (-1, 1), (-1, -1)):
        near.append(
            (dw, dn, {"wide": (w + dw + WIDE) % WIDE, "narrow": (n + dn + NARROW) % NARROW})
        )
    x_dev = [dev(z, (x + d) % 4, core, y) for d in (1, 2, 3)]
    y_dev = [dev(z, x, core, (y + d) % 4) for d in (1, 2, 3)]
    z_dev = [dev((z + d) % 16, x, core, y) for d in range(1, 16)]
    n_dev = [{"wide": w, "narrow": (n + d) % 8} for d in range(1, 8)]

    barrier = pltpu.get_barrier_semaphore()
    partners = [t[2] for t in near] + x_dev + y_dev + z_dev + n_dev
    for p in partners:
        pl.semaphore_signal(barrier, inc=1, device_id=p, device_id_type=MESH)

    c_feat = pltpu.make_async_copy(feat_hbm, halo.at[1:9, 1:9], lsem.at[0])
    c_w = pltpu.make_async_copy(w_hbm, wv, lsem.at[1])
    c_cot = pltpu.make_async_copy(cot_hbm, cot, lsem.at[2])
    c_feat.start()
    c_w.start()
    c_cot.start()

    m = mask_ref[...].astype(F32).reshape(64, 8).astype(BF)
    pick = (iota((512, 64), 0) // 8 == iota((512, 64), 1)).astype(F32).astype(BF)
    mm = jnp.dot(pick, m, preferred_element_type=F32)
    mm = jnp.where(iota((512, 8), 0) % 8 == iota((512, 8), 1), mm, 0.0).astype(BF)
    live[...] = jnp.dot(mm, jnp.ones((8, C), BF), preferred_element_type=F32)

    c_feat.wait()
    for xx in range(8):
        v = halo[1 + xx, 1:9].astype(F32) * live[64 * xx : 64 * xx + 64, :].reshape(8, 8, C)
        halo[1 + xx, 1:9] = v.astype(BF)

    pl.semaphore_wait(barrier, len(partners))

    def exchange(buf, send, recv):
        copies = []
        for k, (dw, dn, d) in enumerate(near):
            sx = {1: slice(8, 9), -1: slice(1, 2), 0: slice(1, 9)}[dw]
            tx = {1: slice(0, 1), -1: slice(9, 10), 0: slice(1, 9)}[dw]
            sy = {1: slice(8, 9), -1: slice(1, 2), 0: slice(1, 9)}[dn]
            ty = {1: slice(0, 1), -1: slice(9, 10), 0: slice(1, 9)}[dn]
            cp = pltpu.make_async_remote_copy(
                src_ref=buf.at[sx, sy],
                dst_ref=buf.at[tx, ty],
                send_sem=send.at[k],
                recv_sem=recv.at[k],
                device_id=d,
                device_id_type=MESH,
            )
            cp.start()
            copies.append(cp)
        return copies

    halo_copies = exchange(halo, hsend, hrecv)
    cols[:, 5120:5248] = jnp.zeros((512, 128), BF)
    for cp in halo_copies:
        cp.wait()

    build_shifts(halo, even, odd, w, n)
    for t in range(27):
        a, b, c = t // 9, (t // 3) % 3, t % 3
        cols[:, C * t : C * t + C] = tap_rows(even, odd, a, b, c)

    c_w.wait()
    pre[...] = jnp.dot(cols[:, 0:5184], wv[...], preferred_element_type=F32)

    c_cot.wait()
    for xx in range(8):
        rows = slice(64 * xx, 64 * xx + 64)
        pv = pre[rows, :]
        lv = live[rows, :]
        sig = jax.nn.sigmoid(pv)
        act_ref[xx] = (pv * sig * lv).reshape(8, 8, C).astype(BF)
        slope = sig * (1.0 + pv * (1.0 - sig))
        ct = cot[xx].astype(F32).reshape(64, C)
        g = ct * lv * slope
        gp2[rows, :] = g.astype(BF)
        ghalo[1 + xx, 1:9] = g.reshape(8, 8, C).astype(BF)

    g_copies = exchange(ghalo, gsend, grecv)

    r = iota((C, C), 0)
    q = (r >= 96).astype(jnp.int32)
    r = r - 96 * q
    rl = (r >= 48).astype(jnp.int32)
    r = r - 48 * rl
    rk = (r >= 16).astype(jnp.int32) + (r >= 32).astype(jnp.int32)
    rz_ = r - 16 * rk
    rc = jnp.where(q == 1, core, 1 - core)
    rj = 3 * ((rz_ * 2 + rl) * 2 + rc) + rk
    perm = (rj == iota((C, C), 1)).astype(F32).astype(BF)
    gpt[...] = lax.dot_general(
        perm, gp2[...], (((1,), (1,)), ((), ())), preferred_element_type=F32
    ).astype(BF)

    tail = jnp.dot(gpt[...], cols[:, 5120:5248], preferred_element_type=F32)
    for l_ in range(2):
        for m_ in range(8):
            k = m_ % 3
            lo = 48 * l_ + 16 * k
            sb[l_, m_ // 2, m_ % 2, 15] = tail[lo : lo + 16].astype(BF)
            own[l_, m_ // 2, m_ % 2, 15] = tail[96 + lo : 112 + lo]

    def owner(i):
        return (y + 2 + 3 * (i // 2)) % 4, (xh + 1 + i) % 2

    partner = dev(z, x, 1 - core, y)

    def core_copy(i):
        yy, hh = owner(i)
        return pltpu.make_async_remote_copy(
            src_ref=sb.at[:, yy, hh],
            dst_ref=rb.at[:, yy, hh],
            send_sem=csend.at[i],
            recv_sem=crecv.at[i],
            device_id=partner,
            device_id_type=MESH,
        )

    def wgrad(i, carry):
        yy, hh = owner(i)
        col = pl.multiple_of((yy * 2 + hh) * 640, 128)
        o = jnp.dot(gpt[...], cols[:, pl.ds(col, 640)], preferred_element_type=F32)
        for l_ in range(2):
            for k in range(3):
                lo = 48 * l_ + 16 * k
                for t in range(5):
                    sb[l_, yy, hh, 5 * k + t] = o[lo : lo + 16, 128 * t : 128 * t + 128].astype(BF)
                    own[l_, yy, hh, 5 * k + t] = o[96 + lo : 112 + lo, 128 * t : 128 * t + 128]
        core_copy(i).start()
        return carry

    lax.fori_loop(0, 8, wgrad, 0)

    def a_copy(i, l_):
        yy, hh = owner(i)
        xt = hh * 2 + l_
        d = (xt - x + 4) % 4
        return d != 0, pltpu.make_async_remote_copy(
            src_ref=s1b.at[l_, yy, hh, pl.ds(0, 8)],
            dst_ref=ra.at[jnp.maximum(d - 1, 0), yy],
            send_sem=asend.at[i, l_],
            recv_sem=arecv.at[jnp.maximum(d - 1, 0), yy],
            device_id=dev(z, xt, core, y),
            device_id_type=MESH,
        )

    def b_copy(i):
        yy, hh = owner(i)
        d = (yy - y + 4) % 4
        return d != 0, pltpu.make_async_remote_copy(
            src_ref=s1b.at[:, yy, hh, pl.ds(8, 8)],
            dst_ref=rby.at[jnp.maximum(d - 1, 0), :, hh],
            send_sem=bsend.at[i],
            recv_sem=brecv.at[jnp.maximum(d - 1, 0), hh],
            device_id=dev(z, x, core, yy),
            device_id_type=MESH,
        )

    def first(i, carry):
        yy, hh = owner(i)
        core_copy(i).wait()
        for l_ in range(2):
            s = own[l_, yy, hh] + rb[l_, yy, hh].astype(F32)
            own[l_, yy, hh] = s
            s1b[l_, yy, hh] = s.astype(BF)
        for l_ in range(2):
            go, cp = a_copy(i, l_)
            pl.when(go)(cp.start)
        go, cp = b_copy(i)
        pl.when(go)(cp.start)
        return carry

    lax.fori_loop(0, 8, first, 0)

    def first_wait(i, carry):
        for l_ in range(2):
            go, cp = a_copy(i, l_)
            pl.when(go)(cp.wait_send)
        go, cp = b_copy(i)
        pl.when(go)(cp.wait_send)
        return carry

    for d in range(3):
        for yy in range(4):
            pltpu.make_async_remote_copy(
                src_ref=s1b.at[0, yy, 0, pl.ds(0, 8)], dst_ref=ra.at[d, yy],
                send_sem=asend.at[0, 0], recv_sem=arecv.at[d, yy],
                device_id=partner, device_id_type=MESH,
            ).wait_recv()
        for hh in range(2):
            pltpu.make_async_remote_copy(
                src_ref=s1b.at[:, 0, hh, pl.ds(8, 8)], dst_ref=rby.at[d, :, hh],
                send_sem=bsend.at[0], recv_sem=brecv.at[d, hh],
                device_id=partner, device_id_type=MESH,
            ).wait_recv()

    for yy in range(4):
        s = own[xl, yy, xh, 0:8]
        for d in range(3):
            s = s + ra[d, yy].astype(F32)
        a1[yy] = s
        a1b[yy] = s.astype(BF)
    for l_ in range(2):
        for hh in range(2):
            s = own[l_, y, hh, 8:16]
            for d in range(3):
                s = s + rby[d, l_, hh].astype(F32)
            b1[hh * 2 + l_] = s
            b1b[hh * 2 + l_] = s.astype(BF)

    second = []
    for d in range(3):
        second.append(
            pltpu.make_async_remote_copy(
                src_ref=a1b.at[(y + d + 1) % 4], dst_ref=ra2.at[d],
                send_sem=a2send.at[d], recv_sem=a2recv.at[d],
                device_id=y_dev[d], device_id_type=MESH,
            )
        )
        second.append(
            pltpu.make_async_remote_copy(
                src_ref=b1b.at[(x + d + 1) % 4], dst_ref=rb2.at[d],
                send_sem=b2send.at[d], recv_sem=b2recv.at[d],
                device_id=x_dev[d], device_id_type=MESH,
            )
        )
    for cp in second:
        cp.start()
    lax.fori_loop(0, 8, first_wait, 0)
    for cp in second:
        cp.wait()
    sa = a1[y]
    sbb = b1[x]
    for d in range(3):
        sa = sa + ra2[d].astype(F32)
        sbb = sbb + rb2[d].astype(F32)
    tb[0:128] = sa.reshape(128, 128).astype(BF)
    tb[128:256] = sbb.reshape(128, 128).astype(BF)

    rr = iota((256, 256), 0)
    turn = (iota((256, 256), 1) == (rr % 16) * 16 + rr // 16).astype(F32).astype(BF)
    zb[...] = (
        jnp.dot(turn, tb[...], preferred_element_type=F32).astype(BF).reshape(16, 16, 128)
    )
    z_copies = []
    for d in range(15):
        cp = pltpu.make_async_remote_copy(
            src_ref=zb.at[(z + d + 1) % 16], dst_ref=rz.at[d],
            send_sem=zsend.at[d], recv_sem=zrecv.at[d],
            device_id=z_dev[d], device_id_type=MESH,
        )
        z_copies.append(cp)
    for d in (7, 6, 8, 5, 9, 4, 10, 3, 11, 2, 12, 1, 13, 0, 14):
        z_copies[d].start()

    for cp in g_copies:
        cp.wait()
    build_shifts(ghalo, even, odd, w, n)
    pre[...] = jnp.zeros((512, C), F32)
    for t in range(27):
        a, b, c = t // 9, (t // 3) % 3, t % 3
        pre[...] += lax.dot_general(
            tap_rows(even, odd, 2 - a, 2 - b, 2 - c),
            wv[C * t : C * t + C, :],
            (((1,), (1,)), ((), ())),
            preferred_element_type=F32,
        )
    for xx in range(8):
        rows = slice(64 * xx, 64 * xx + 64)
        gin_ref[xx] = (pre[rows, :] * live[rows, :]).reshape(8, 8, C).astype(BF)

    total = zb[z].astype(F32)
    for d in range(15):
        z_copies[d].wait()
        total = total + rz[d].astype(F32)
    fin[...] = total * (1.0 / 512.0)

    g_all = []
    for d in range(7):
        cp = pltpu.make_async_remote_copy(
            src_ref=fin, dst_ref=ag.at[n],
            send_sem=gsnd.at[d], recv_sem=grcv.at[d],
            device_id=n_dev[d], device_id_type=MESH,
        )
        cp.start()
        g_all.append(cp)
    ag[n] = fin[...]
    for cp in g_all:
        cp.wait()
    for m_ in range(8):
        for k in range(3):
            for t in range(5):
                lo = (5 * m_ + t) * 128
                gw_ref[k : k + 1, lo : lo + 128] = ag[m_, 5 * k + t : 5 * k + t + 1, :]
    for k in range(3):
        gw_ref[k : k + 1, 5120:5184] = ag[k, 15:16, 0:64]


def local(features, weight, voxel_mask, cotangent):
    dma = pltpu.SemaphoreType.DMA
    vmem = pltpu.VMEM
    scratch = [
        vmem((27 * C, C), BF),
        vmem((8, 8, 8, C), BF),
        vmem((10, 10, 8, C), BF),
        vmem((10, 10, 8, C), BF),
        vmem((3, 10, 80, C), BF),
        vmem((3, 10, 64, C), BF),
        vmem((512, 5248), BF),
        vmem((512, C), F32),
        vmem((512, C), F32),
        vmem((512, C), BF),
        vmem((C, 512), BF),
        vmem((2, 4, 2, 16, 16, 128), F32),
        vmem((2, 4, 2, 16, 16, 128), BF),
        vmem((2, 4, 2, 16, 16, 128), BF),
        vmem((2, 4, 2, 16, 16, 128), BF),
        vmem((4, 8, 16, 128), F32),
        vmem((4, 8, 16, 128), F32),
        vmem((4, 8, 16, 128), BF),
        vmem((4, 8, 16, 128), BF),
        vmem((256, 128), BF),
        vmem((16, 16, 128), BF),
        vmem((16, 128), F32),
        vmem((3, 4, 8, 16, 128), BF),
        vmem((3, 2, 2, 8, 16, 128), BF),
        vmem((3, 8, 16, 128), BF),
        vmem((3, 8, 16, 128), BF),
        vmem((15, 16, 128), BF),
        vmem((8, 16, 128), F32),
        dma((3,)),
        dma((8,)), dma((8,)), dma((8,)), dma((8,)),
        dma((8,)), dma((8,)),
        dma((8, 2)), dma((3, 4)),
        dma((8,)), dma((3, 2)),
        dma((3,)), dma((3,)), dma((3,)), dma((3,)),
        dma((15,)), dma((15,)),
        dma((7,)), dma((7,)),
    ]
    any_ = pl.BlockSpec(memory_space=pl.ANY)
    vm = pl.BlockSpec(memory_space=pltpu.VMEM)
    return pl.pallas_call(
        kernel,
        name="sparse_conv",
        out_shape=(
            jax.ShapeDtypeStruct((8, 8, 8, C), BF),
            jax.ShapeDtypeStruct((8, 8, 8, C), BF),
            jax.ShapeDtypeStruct((3, 27 * C), F32),
        ),
        in_specs=[any_, any_, vm, any_],
        out_specs=(vm, vm, vm),
        scratch_shapes=scratch,
        compiler_params=pltpu.CompilerParams(
            collective_id=0, has_side_effects=True, vmem_limit_bytes=60 * 1024 * 1024
        ),
    )(features, weight, voxel_mask, cotangent)


def solution(mesh):
    return jax.shard_map(
        local,
        mesh=mesh,
        in_specs=(
            P("wide", "narrow", None, None),
            P(),
            P("wide", "narrow", None),
            P("wide", "narrow", None, None),
        ),
        out_specs=(
            P("wide", "narrow", None, None),
            P("wide", "narrow", None, None),
            P("wide", None),
        ),
        check_vma=False,
    )
```

time: 579 us -> 64.1 us (0.11)
  the two profiles are of different devices: /device:TPU:8 before, /device:TPU:2 now
where the time goes in v1:
time: 64.1 us; the launch traced here: 63.8 us
  Pallas kernels  54 us (84%)
  local copies, waits for them, and re-layouts  9.16 us (14%)
    pallas_call x1, Pallas kernels, local(): pl.pallas_call(kernel, name='sparse_conv', out_shape=(jax.ShapeDtypeStruc...  54 us
    unnamed x4, local copies, waits for them, and re-layouts  9.16 us

profile of v1, /device:TPU:2, one launch (start us, length us, event | category | flops | bytes accessed | tf_op | source)
XLA Modules:
  0.0 63.8 jit_solution(14338059301868470882)
XLA Ops:
  0.6 4.3 %copy.7.w_hbm = bf16[5184,192]{1,0:T(8,128)(2,1)} copy(bf16[5184,192]{0,1:T(8,128)(2,1)} %param.5) | data formatting | bytes 3981312 | tf_op args[1]
  4.9 54.0 %sparse_conv.1 = (bf16[8,8,8,192]{3,2,1,0:T(8,128)(2,1)}, bf16[8,8,8,192]{3,2,1,0:T(8,128)(2,1)}, f32[3,5184]{1,0:T(4,128)}) custom-call(bf16[8,8,8,192]{3,2,1,0:T(8,128)(2,1)} %feat_hbm.1, bf16[5184,192]{1,0:T(8,128)(2,1)} %copy.7.w_hbm, s32[8,8,8]{2,1,0:T(8,128)} %mask_ref.1, bf16[8,8,8,192]{3,2,1,0:T(8,128)(2,1)} %cot_hbm.1), custom_call_target="tpu_custom_call" | custom-call | tf_op jit(solution)/shard_map/sparse_conv/pallas_call | solution.py:419
  58.9 1.7 %copy.11 = bf16[8,8,8,192]{3,2,1,0:T(8,128)(2,1)} copy(bf16[8,8,8,192]{3,2,1,0:T(8,128)(2,1)} %get-tuple-element.6) | data formatting | bytes 393216
  60.6 1.7 %copy.12 = bf16[8,8,8,192]{3,2,1,0:T(8,128)(2,1)} copy(bf16[8,8,8,192]{3,2,1,0:T(8,128)(2,1)} %get-tuple-element.7) | data formatting | bytes 393216
  62.2 1.5 %copy.13 = f32[3,5184]{1,0:T(4,128)} copy(f32[3,5184]{1,0:T(4,128)} %get-tuple-element.8) | data formatting | bytes 124416

commit v2 on v1

--- a/solution.py
+++ b/solution.py
@@ -10,6 +10,7 @@
 F32 = jnp.float32
 MESH = pl.DeviceIdType.MESH
 WIDE, NARROW = 64, 8
+LAG = 3
 
 
 def iota(shape, dim):
@@ -52,14 +53,14 @@
 
 
 def kernel(
-    feat_hbm, w_hbm, mask_ref, cot_hbm,
-    act_ref, gin_ref, gw_ref,
-    wv, cot, halo, ghalo, even, odd, cols, pre, live, gp2, gpt,
+    feat_hbm, w_hbm, mask_hbm, cot_hbm,
+    act_ref, gin_ref, ag,
+    wv, mask, cot, halo, ghalo, even, odd, cols, pre, live, gp2, gpt,
     own, sb, rb, s1b, a1, b1, a1b, b1b, tb, zb, fin,
-    ra, rby, ra2, rb2, rz, ag,
+    ra, rby, ra2, rb2, rz,
     lsem, hsend, hrecv, gsend, grecv, csend, crecv,
     asend, arecv, bsend, brecv, a2send, a2recv, b2send, b2recv,
-    zsend, zrecv, gsnd, grcv,
+    zsend, zrecv, gsnd, grcv, ring,
 ):
     w = lax.axis_index("wide")
     n = lax.axis_index("narrow")
@@ -84,18 +85,21 @@
     n_dev = [{"wide": w, "narrow": (n + d) % 8} for d in range(1, 8)]
 
     barrier = pltpu.get_barrier_semaphore()
-    partners = [t[2] for t in near] + x_dev + y_dev + z_dev + n_dev
+    partners = [t[2] for t in near] + n_dev + x_dev + [z_dev[0], z_dev[14]]
     for p in partners:
         pl.semaphore_signal(barrier, inc=1, device_id=p, device_id_type=MESH)
 
     c_feat = pltpu.make_async_copy(feat_hbm, halo.at[1:9, 1:9], lsem.at[0])
     c_w = pltpu.make_async_copy(w_hbm, wv, lsem.at[1])
     c_cot = pltpu.make_async_copy(cot_hbm, cot, lsem.at[2])
+    c_mask = pltpu.make_async_copy(mask_hbm, mask, lsem.at[3])
+    c_mask.start()
     c_feat.start()
     c_w.start()
     c_cot.start()
 
-    m = mask_ref[...].astype(F32).reshape(64, 8).astype(BF)
+    c_mask.wait()
+    m = mask[...].astype(F32).reshape(64, 8).astype(BF)
     pick = (iota((512, 64), 0) // 8 == iota((512, 64), 1)).astype(F32).astype(BF)
     mm = jnp.dot(pick, m, preferred_element_type=F32)
     mm = jnp.where(iota((512, 8), 0) % 8 == iota((512, 8), 1), mm, 0.0).astype(BF)
@@ -107,6 +111,15 @@
         halo[1 + xx, 1:9] = v.astype(BF)
 
     pl.semaphore_wait(barrier, len(partners))
+
+    def tell(d, k):
+        for p in (z_dev[d - 1], z_dev[15 - d]):
+            pl.semaphore_signal(ring.at[k], inc=1, device_id=p, device_id_type=MESH)
+
+    def met(k):
+        pl.semaphore_wait(ring.at[k], 2)
+
+    tell(1, 0)
 
     def exchange(buf, send, recv):
         copies = []
@@ -131,6 +144,8 @@
     cols[:, 5120:5248] = jnp.zeros((512, 128), BF)
     for cp in halo_copies:
         cp.wait()
+    met(0)
+    tell(2, 1)
 
     build_shifts(halo, even, odd, w, n)
     for t in range(27):
@@ -138,8 +153,12 @@
         cols[:, C * t : C * t + C] = tap_rows(even, odd, a, b, c)
 
     c_w.wait()
-    pre[...] = jnp.dot(cols[:, 0:5184], wv[...], preferred_element_type=F32)
-
+    pre[...] = lax.dot_general(
+        cols[:, 0:5184], wv[...], (((1,), (1,)), ((), ())), preferred_element_type=F32
+    )
+
+    met(1)
+    tell(4, 2)
     c_cot.wait()
     for xx in range(8):
         rows = slice(64 * xx, 64 * xx + 64)
@@ -206,8 +225,6 @@
         core_copy(i).start()
         return carry
 
-    lax.fori_loop(0, 8, wgrad, 0)
-
     def a_copy(i, l_):
         yy, hh = owner(i)
         xt = hh * 2 + l_
@@ -247,8 +264,14 @@
         pl.when(go)(cp.start)
         return carry
 
-    lax.fori_loop(0, 8, first, 0)
-
+    def both(i, carry):
+        wgrad(i, carry)
+        first(i - LAG, carry)
+        return carry
+
+    lax.fori_loop(0, LAG, wgrad, 0)
+    lax.fori_loop(LAG, 8, both, 0)
+    lax.fori_loop(8 - LAG, 8, first, 0)
     def first_wait(i, carry):
         for l_ in range(2):
             go, cp = a_copy(i, l_)
@@ -303,6 +326,7 @@
         )
     for cp in second:
         cp.start()
+    met(2)
     lax.fori_loop(0, 8, first_wait, 0)
     for cp in second:
         cp.wait()
@@ -336,10 +360,9 @@
     pre[...] = jnp.zeros((512, C), F32)
     for t in range(27):
         a, b, c = t // 9, (t // 3) % 3, t % 3
-        pre[...] += lax.dot_general(
+        pre[...] += jnp.dot(
             tap_rows(even, odd, 2 - a, 2 - b, 2 - c),
-            wv[C * t : C * t + C, :],
-            (((1,), (1,)), ((), ())),
+            wv[:, C * t : C * t + C],
             preferred_element_type=F32,
         )
     for xx in range(8):
@@ -364,20 +387,37 @@
     ag[n] = fin[...]
     for cp in g_all:
         cp.wait()
+
+
+def finish(act_in, gin_in, ag_in, act_out, gin_out, gw_out, ag, gw, sem):
+    copies = [
+        pltpu.make_async_copy(ag_in, ag, sem.at[0]),
+        pltpu.make_async_copy(act_in, act_out, sem.at[1]),
+        pltpu.make_async_copy(gin_in, gin_out, sem.at[2]),
+    ]
+    for cp in copies:
+        cp.start()
+    copies[0].wait()
     for m_ in range(8):
         for k in range(3):
             for t in range(5):
                 lo = (5 * m_ + t) * 128
-                gw_ref[k : k + 1, lo : lo + 128] = ag[m_, 5 * k + t : 5 * k + t + 1, :]
+                gw[k : k + 1, lo : lo + 128] = ag[m_, 5 * k + t : 5 * k + t + 1, :]
     for k in range(3):
-        gw_ref[k : k + 1, 5120:5184] = ag[k, 15:16, 0:64]
+        gw[k : k + 1, 5120:5184] = ag[k, 15:16, 0:64]
+    cp = pltpu.make_async_copy(gw, gw_out, sem.at[3])
+    cp.start()
+    copies[1].wait()
+    copies[2].wait()
+    cp.wait()
 
 
 def local(features, weight, voxel_mask, cotangent):
     dma = pltpu.SemaphoreType.DMA
     vmem = pltpu.VMEM
     scratch = [
-        vmem((27 * C, C), BF),
+        vmem((C, 27 * C), BF),
+        vmem((8, 8, 8), jnp.int32),
         vmem((8, 8, 8, C), BF),
         vmem((10, 10, 8, C), BF),
         vmem((10, 10, 8, C), BF),
@@ -404,8 +444,7 @@
         vmem((3, 8, 16, 128), BF),
         vmem((3, 8, 16, 128), BF),
         vmem((15, 16, 128), BF),
-        vmem((8, 16, 128), F32),
-        dma((3,)),
+        dma((4,)),
         dma((8,)), dma((8,)), dma((8,)), dma((8,)),
         dma((8,)), dma((8,)),
         dma((8, 2)), dma((3, 4)),
@@ -413,24 +452,39 @@
         dma((3,)), dma((3,)), dma((3,)), dma((3,)),
         dma((15,)), dma((15,)),
         dma((7,)), dma((7,)),
+        pltpu.SemaphoreType.REGULAR((3,)),
     ]
     any_ = pl.BlockSpec(memory_space=pl.ANY)
+    hbm = pl.BlockSpec(memory_space=pltpu.HBM)
     vm = pl.BlockSpec(memory_space=pltpu.VMEM)
-    return pl.pallas_call(
+    act, gin, blocks = pl.pallas_call(
         kernel,
         name="sparse_conv",
+        out_shape=(
+            pltpu.VMEM((8, 8, 8, C), BF),
+            pltpu.VMEM((8, 8, 8, C), BF),
+            pltpu.VMEM((8, 16, 128), F32),
+        ),
+        in_specs=[hbm] * 4,
+        out_specs=(vm, vm, vm),
+        scratch_shapes=scratch,
+        compiler_params=pltpu.CompilerParams(
+            collective_id=0, has_side_effects=True, vmem_limit_bytes=61 * 1024 * 1024
+        ),
+    )(features, weight.T, voxel_mask, cotangent)
+    return pl.pallas_call(
+        finish,
+        name="finish",
         out_shape=(
             jax.ShapeDtypeStruct((8, 8, 8, C), BF),
             jax.ShapeDtypeStruct((8, 8, 8, C), BF),
             jax.ShapeDtypeStruct((3, 27 * C), F32),
         ),
-        in_specs=[any_, any_, vm, any_],
-        out_specs=(vm, vm, vm),
-        scratch_shapes=scratch,
-        compiler_params=pltpu.CompilerParams(
-            collective_id=0, has_side_effects=True, vmem_limit_bytes=60 * 1024 * 1024
-        ),
-    )(features, weight, voxel_mask, cotangent)
+        in_specs=[any_] * 3,
+        out_specs=(any_, any_, any_),
+        scratch_shapes=[vmem((8, 16, 128), F32), vmem((3, 27 * C), F32), dma((4,))],
+        compiler_params=pltpu.CompilerParams(vmem_limit_bytes=4 * 1024 * 1024),
+    )(act, gin, blocks)
 
 
 def solution(mesh):

time: 64.1 us -> 53.1 us (0.83)
  the two profiles are of different devices: /device:TPU:2 before, /device:TPU:8 now
where the time goes in v2:
time: 53.1 us; the launch traced here: 53 us
  Pallas kernels  52.3 us (98%)
  between operations  0.64 us (1%)
    pallas_call x1, Pallas kernels, local(): pl.pallas_call(kernel, name='sparse_conv', out_shape=(pltpu.VMEM((8, 8, 8...  51.4 us

profile of v2, /device:TPU:8, one launch (start us, length us, event | category | flops | bytes accessed | tf_op | source)
XLA Modules:
  0.0 53.0 jit_solution(10654803096060876886)
XLA Ops:
  0.6 51.4 %sparse_conv.1 = (bf16[8,8,8,192]{3,2,1,0:T(8,128)(2,1)S(1)}, bf16[8,8,8,192]{3,2,1,0:T(8,128)(2,1)S(1)}, f32[8,16,128]{2,1,0:T(8,128)S(1)}) custom-call(bf16[8,8,8,192]{3,2,1,0:T(8,128)(2,1)} %feat_hbm.1, bf16[192,5184]{1,0:T(8,128)(2,1)} %bitcast.1, s32[8,8,8]{2,1,0:T(8,128)} %mask_hbm.1, bf16[8,8,8,192]{3,2,1,0:T(8,128)(2,1)} %cot_hbm.1), custom_call_target="tpu_custom_call" | custom-call | tf_op jit(solution)/shard_map/sparse_conv/pallas_call | solution.py:460
  52.1 0.9 %finish.1 = (bf16[8,8,8,192]{3,2,1,0:T(8,128)(2,1)}, bf16[8,8,8,192]{3,2,1,0:T(8,128)(2,1)}, f32[3,5184]{1,0:T(4,128)}) custom-call(bf16[8,8,8,192]{3,2,1,0:T(8,128)(2,1)S(1)} %get-tuple-element.6.act_in, bf16[8,8,8,192]{3,2,1,0:T(8,128)(2,1)S(1)} %get-tuple-element.7.gin_in, f32[8,16,128]{2,1,0:T(8,128)S(1)} %get-tuple-element.8.ag_in), custom_call_target="tpu_custom_call" | custom-call | tf_op jit(solution)/shard_map/finish/pallas_call | solution.py:475

commit v3 on v2

--- a/solution.py
+++ b/solution.py
@@ -57,9 +57,9 @@
     act_ref, gin_ref, ag,
     wv, mask, cot, halo, ghalo, even, odd, cols, pre, live, gp2, gpt,
     own, sb, rb, s1b, a1, b1, a1b, b1b, tb, zb, fin,
-    ra, rby, ra2, rb2, rz,
+    fl, fr, fd, fu, rpa, rma, rpb, rmb, ra2, rb2, rz, permv, turnv,
     lsem, hsend, hrecv, gsend, grecv, csend, crecv,
-    asend, arecv, bsend, brecv, a2send, a2recv, b2send, b2recv,
+    ads, adr, ars, arr, ass, asr, bds, bdr, brs, brr, bss, bsr, a2send, a2recv, b2send, b2recv,
     zsend, zrecv, gsnd, grcv, ring,
 ):
     w = lax.axis_index("wide")
@@ -75,7 +75,7 @@
         return {"wide": (z_ * 2 + x_ % 2) * 2 + c_, "narrow": y_ * 2 + x_ // 2}
 
     near = []
-    for dw, dn in ((1, 0), (-1, 0), (0, 1), (0, -1), (1, 1), (1, -1), (-1, 1), (-1, -1)):
+    for dw, dn in ((1, 1), (1, -1), (-1, 1), (-1, -1), (0, 1), (0, -1), (1, 0), (-1, 0)):
         near.append(
             (dw, dn, {"wide": (w + dw + WIDE) % WIDE, "narrow": (n + dn + NARROW) % NARROW})
         )
@@ -142,6 +142,19 @@
 
     halo_copies = exchange(halo, hsend, hrecv)
     cols[:, 5120:5248] = jnp.zeros((512, 128), BF)
+    r = iota((C, C), 0)
+    q = (r >= 96).astype(jnp.int32)
+    r = r - 96 * q
+    rl = (r >= 48).astype(jnp.int32)
+    r = r - 48 * rl
+    rk = (r >= 16).astype(jnp.int32) + (r >= 32).astype(jnp.int32)
+    rz_ = r - 16 * rk
+    rc = jnp.where(q == 1, core, 1 - core)
+    rj = 3 * ((rz_ * 2 + rl) * 2 + rc) + rk
+    permv[...] = (rj == iota((C, C), 1)).astype(F32).astype(BF)
+    rr = iota((256, 256), 0)
+    turnv[...] = (iota((256, 256), 1) == (rr % 16) * 16 + rr // 16).astype(F32).astype(BF)
+
     for cp in halo_copies:
         cp.wait()
     met(0)
@@ -174,18 +187,8 @@
 
     g_copies = exchange(ghalo, gsend, grecv)
 
-    r = iota((C, C), 0)
-    q = (r >= 96).astype(jnp.int32)
-    r = r - 96 * q
-    rl = (r >= 48).astype(jnp.int32)
-    r = r - 48 * rl
-    rk = (r >= 16).astype(jnp.int32) + (r >= 32).astype(jnp.int32)
-    rz_ = r - 16 * rk
-    rc = jnp.where(q == 1, core, 1 - core)
-    rj = 3 * ((rz_ * 2 + rl) * 2 + rc) + rk
-    perm = (rj == iota((C, C), 1)).astype(F32).astype(BF)
     gpt[...] = lax.dot_general(
-        perm, gp2[...], (((1,), (1,)), ((), ())), preferred_element_type=F32
+        permv[...], gp2[...], (((1,), (1,)), ((), ())), preferred_element_type=F32
     ).astype(BF)
 
     tail = jnp.dot(gpt[...], cols[:, 5120:5248], preferred_element_type=F32)
@@ -197,7 +200,7 @@
             own[l_, m_ // 2, m_ % 2, 15] = tail[96 + lo : 112 + lo]
 
     def owner(i):
-        return (y + 2 + 3 * (i // 2)) % 4, (xh + 1 + i) % 2
+        return (y + 2 + 3 * (i % 4)) % 4, (xh + 1 + i // 4) % 2
 
     partner = dev(z, x, 1 - core, y)
 
@@ -225,30 +228,53 @@
         core_copy(i).start()
         return carry
 
-    def a_copy(i, l_):
-        yy, hh = owner(i)
-        xt = hh * 2 + l_
-        d = (xt - x + 4) % 4
-        return d != 0, pltpu.make_async_remote_copy(
-            src_ref=s1b.at[l_, yy, hh, pl.ds(0, 8)],
-            dst_ref=ra.at[jnp.maximum(d - 1, 0), yy],
-            send_sem=asend.at[i, l_],
-            recv_sem=arecv.at[jnp.maximum(d - 1, 0), yy],
-            device_id=dev(z, xt, core, y),
-            device_id_type=MESH,
-        )
-
-    def b_copy(i):
-        yy, hh = owner(i)
-        d = (yy - y + 4) % 4
-        return d != 0, pltpu.make_async_remote_copy(
-            src_ref=s1b.at[:, yy, hh, pl.ds(8, 8)],
-            dst_ref=rby.at[jnp.maximum(d - 1, 0), :, hh],
-            send_sem=bsend.at[i],
-            recv_sem=brecv.at[jnp.maximum(d - 1, 0), hh],
-            device_id=dev(z, x, core, yy),
-            device_id_type=MESH,
-        )
+    xp, xo, xm = (x + 1) % 4, (x + 2) % 4, (x + 3) % 4
+    yp, yo, ym = (y + 1) % 4, (y + 2) % 4, (y + 3) % 4
+
+    def remote(src, dst, send, recv, d):
+        return pltpu.make_async_remote_copy(
+            src_ref=src, dst_ref=dst, send_sem=send, recv_sem=recv,
+            device_id=d, device_id_type=MESH,
+        )
+
+    def a_part(xt, yy, lo):
+        return s1b.at[xt % 2, yy, xt // 2, pl.ds(lo, 4)]
+
+    def a_dir(yy):
+        return (
+            remote(a_part(xp, yy, 4), fl.at[yy, pl.ds(4, 4)], ads.at[0, yy], adr.at[0, yy], x_dev[0]),
+            remote(a_part(xm, yy, 0), fr.at[yy, pl.ds(0, 4)], ads.at[1, yy], adr.at[1, yy], x_dev[2]),
+        )
+
+    def a_rel(yy):
+        return (
+            remote(a_part(xo, yy, 0), rpa.at[yy], ars.at[0, yy], arr.at[0, yy], x_dev[0]),
+            remote(a_part(xo, yy, 4), rma.at[yy], ars.at[1, yy], arr.at[1, yy], x_dev[2]),
+        )
+
+    def b_part(yt, hh, lo):
+        return s1b.at[:, yt, hh, pl.ds(lo, 4)]
+
+    def b_dir(hh):
+        return (
+            remote(b_part(yp, hh, 12), fd.at[:, hh, pl.ds(4, 4)], bds.at[0, hh], bdr.at[0, hh], y_dev[0]),
+            remote(b_part(ym, hh, 8), fu.at[:, hh, pl.ds(0, 4)], bds.at[1, hh], bdr.at[1, hh], y_dev[2]),
+        )
+
+    def b_rel(hh):
+        return (
+            remote(b_part(yo, hh, 8), rpb.at[hh], brs.at[0, hh], brr.at[0, hh], y_dev[0]),
+            remote(b_part(yo, hh, 12), rmb.at[hh], brs.at[1, hh], brr.at[1, hh], y_dev[2]),
+        )
+
+    a_sum = (
+        remote(s1b.at[xp % 2, :, xp // 2, pl.ds(0, 4)], fl.at[:, pl.ds(0, 4)], ass.at[0], asr.at[0], x_dev[0]),
+        remote(s1b.at[xm % 2, :, xm // 2, pl.ds(4, 4)], fr.at[:, pl.ds(4, 4)], ass.at[1], asr.at[1], x_dev[2]),
+    )
+    b_sum = (
+        remote(s1b.at[:, yp, :, pl.ds(8, 4)], fd.at[:, :, pl.ds(0, 4)], bss.at[0], bsr.at[0], y_dev[0]),
+        remote(s1b.at[:, ym, :, pl.ds(12, 4)], fu.at[:, :, pl.ds(4, 4)], bss.at[1], bsr.at[1], y_dev[2]),
+    )
 
     def first(i, carry):
         yy, hh = owner(i)
@@ -258,10 +284,13 @@
             own[l_, yy, hh] = s
             s1b[l_, yy, hh] = s.astype(BF)
         for l_ in range(2):
-            go, cp = a_copy(i, l_)
-            pl.when(go)(cp.start)
-        go, cp = b_copy(i)
-        pl.when(go)(cp.start)
+            xt = hh * 2 + l_
+            pl.when(xt == xo)(lambda: [cp.start() for cp in a_rel(yy)] and None)
+            pl.when(xt == xp)(a_dir(yy)[0].start)
+            pl.when(xt == xm)(a_dir(yy)[1].start)
+        pl.when(yy == yo)(lambda: [cp.start() for cp in b_rel(hh)] and None)
+        pl.when(yy == yp)(b_dir(hh)[0].start)
+        pl.when(yy == ym)(b_dir(hh)[1].start)
         return carry
 
     def both(i, carry):
@@ -272,39 +301,43 @@
     lax.fori_loop(0, LAG, wgrad, 0)
     lax.fori_loop(LAG, 8, both, 0)
     lax.fori_loop(8 - LAG, 8, first, 0)
-    def first_wait(i, carry):
+    for yy in range(4):
+        for cp in a_rel(yy):
+            cp.wait_recv()
+        s = own[xp % 2, yy, xp // 2, 0:4] + rpa[yy].astype(F32)
+        s1b[xp % 2, yy, xp // 2, 0:4] = s.astype(BF)
+        s = own[xm % 2, yy, xm // 2, 4:8] + rma[yy].astype(F32)
+        s1b[xm % 2, yy, xm // 2, 4:8] = s.astype(BF)
+    for cp in a_sum:
+        cp.start()
+    for hh in range(2):
+        for cp in b_rel(hh):
+            cp.wait_recv()
         for l_ in range(2):
-            go, cp = a_copy(i, l_)
-            pl.when(go)(cp.wait_send)
-        go, cp = b_copy(i)
-        pl.when(go)(cp.wait_send)
-        return carry
-
-    for d in range(3):
-        for yy in range(4):
-            pltpu.make_async_remote_copy(
-                src_ref=s1b.at[0, yy, 0, pl.ds(0, 8)], dst_ref=ra.at[d, yy],
-                send_sem=asend.at[0, 0], recv_sem=arecv.at[d, yy],
-                device_id=partner, device_id_type=MESH,
-            ).wait_recv()
-        for hh in range(2):
-            pltpu.make_async_remote_copy(
-                src_ref=s1b.at[:, 0, hh, pl.ds(8, 8)], dst_ref=rby.at[d, :, hh],
-                send_sem=bsend.at[0], recv_sem=brecv.at[d, hh],
-                device_id=partner, device_id_type=MESH,
-            ).wait_recv()
+            s = own[l_, yp, hh, 8:12] + rpb[hh, l_].astype(F32)
+            s1b[l_, yp, hh, 8:12] = s.astype(BF)
+            s = own[l_, ym, hh, 12:16] + rmb[hh, l_].astype(F32)
+            s1b[l_, ym, hh, 12:16] = s.astype(BF)
+    for cp in b_sum:
+        cp.start()
 
     for yy in range(4):
-        s = own[xl, yy, xh, 0:8]
-        for d in range(3):
-            s = s + ra[d, yy].astype(F32)
+        for cp in a_dir(yy):
+            cp.wait_recv()
+    for cp in a_sum:
+        cp.wait_recv()
+    for yy in range(4):
+        s = own[xl, yy, xh, 0:8] + fl[yy].astype(F32) + fr[yy].astype(F32)
         a1[yy] = s
         a1b[yy] = s.astype(BF)
+    for hh in range(2):
+        for cp in b_dir(hh):
+            cp.wait_recv()
+    for cp in b_sum:
+        cp.wait_recv()
     for l_ in range(2):
         for hh in range(2):
-            s = own[l_, y, hh, 8:16]
-            for d in range(3):
-                s = s + rby[d, l_, hh].astype(F32)
+            s = own[l_, y, hh, 8:16] + fd[l_, hh].astype(F32) + fu[l_, hh].astype(F32)
             b1[hh * 2 + l_] = s
             b1b[hh * 2 + l_] = s.astype(BF)
 
@@ -327,7 +360,13 @@
     for cp in second:
         cp.start()
     met(2)
-    lax.fori_loop(0, 8, first_wait, 0)
+    sent = list(a_sum) + list(b_sum)
+    for k in range(4):
+        sent += list(a_dir(k)) + list(a_rel(k))
+    for k in range(2):
+        sent += list(b_dir(k)) + list(b_rel(k))
+    for cp in sent:
+        cp.wait_send()
     for cp in second:
         cp.wait()
     sa = a1[y]
@@ -338,10 +377,8 @@
     tb[0:128] = sa.reshape(128, 128).astype(BF)
     tb[128:256] = sbb.reshape(128, 128).astype(BF)
 
-    rr = iota((256, 256), 0)
-    turn = (iota((256, 256), 1) == (rr % 16) * 16 + rr // 16).astype(F32).astype(BF)
     zb[...] = (
-        jnp.dot(turn, tb[...], preferred_element_type=F32).astype(BF).reshape(16, 16, 128)
+        jnp.dot(turnv[...], tb[...], preferred_element_type=F32).astype(BF).reshape(16, 16, 128)
     )
     z_copies = []
     for d in range(15):
@@ -439,16 +476,19 @@
         vmem((256, 128), BF),
         vmem((16, 16, 128), BF),
         vmem((16, 128), F32),
-        vmem((3, 4, 8, 16, 128), BF),
-        vmem((3, 2, 2, 8, 16, 128), BF),
+        vmem((4, 8, 16, 128), BF), vmem((4, 8, 16, 128), BF),
+        vmem((2, 2, 8, 16, 128), BF), vmem((2, 2, 8, 16, 128), BF),
+        vmem((4, 4, 16, 128), BF), vmem((4, 4, 16, 128), BF),
+        vmem((2, 2, 4, 16, 128), BF), vmem((2, 2, 4, 16, 128), BF),
         vmem((3, 8, 16, 128), BF),
         vmem((3, 8, 16, 128), BF),
         vmem((15, 16, 128), BF),
+        vmem((C, C), BF), vmem((256, 256), BF),
         dma((4,)),
         dma((8,)), dma((8,)), dma((8,)), dma((8,)),
         dma((8,)), dma((8,)),
-        dma((8, 2)), dma((3, 4)),
-        dma((8,)), dma((3, 2)),
+        dma((2, 4)), dma((2, 4)), dma((2, 4)), dma((2, 4)), dma((2,)), dma((2,)),
+        dma((2, 2)), dma((2, 2)), dma((2, 2)), dma((2, 2)), dma((2,)), dma((2,)),
         dma((3,)), dma((3,)), dma((3,)), dma((3,)),
         dma((15,)), dma((15,)),
         dma((7,)), dma((7,)),

time: 53.1 us -> 53.5 us (level)
  the two profiles are of different devices: /device:TPU:8 before, /device:TPU:32 now
where the time goes in v3:
time: 53.5 us; the launch traced here: 53.4 us
  Pallas kernels  52.7 us (99%)
  between operations  0.64 us (1%)
    pallas_call x1, Pallas kernels, local(): pl.pallas_call(kernel, name='sparse_conv', out_shape=(pltpu.VMEM((8, 8, 8...  51.8 us

profile of v3, /device:TPU:32, one launch (start us, length us, event | category | flops | bytes accessed | tf_op | source)
XLA Modules:
  0.0 53.4 jit_solution(364112689116304203)
XLA Ops:
  0.6 51.8 %sparse_conv.1 = (bf16[8,8,8,192]{3,2,1,0:T(8,128)(2,1)S(1)}, bf16[8,8,8,192]{3,2,1,0:T(8,128)(2,1)S(1)}, f32[8,16,128]{2,1,0:T(8,128)S(1)}) custom-call(bf16[8,8,8,192]{3,2,1,0:T(8,128)(2,1)} %feat_hbm.1, bf16[192,5184]{1,0:T(8,128)(2,1)} %bitcast.1, s32[8,8,8]{2,1,0:T(8,128)} %mask_hbm.1, bf16[8,8,8,192]{3,2,1,0:T(8,128)(2,1)} %cot_hbm.1), custom_call_target="tpu_custom_call" | custom-call | tf_op jit(solution)/shard_map/sparse_conv/pallas_call | solution.py:500
  52.4 0.9 %finish.1 = (bf16[8,8,8,192]{3,2,1,0:T(8,128)(2,1)}, bf16[8,8,8,192]{3,2,1,0:T(8,128)(2,1)}, f32[3,5184]{1,0:T(4,128)}) custom-call(bf16[8,8,8,192]{3,2,1,0:T(8,128)(2,1)S(1)} %get-tuple-element.6.act_in, bf16[8,8,8,192]{3,2,1,0:T(8,128)(2,1)S(1)} %get-tuple-element.7.gin_in, f32[8,16,128]{2,1,0:T(8,128)S(1)} %get-tuple-element.8.ag_in), custom_call_target="tpu_custom_call" | custom-call | tf_op jit(solution)/shard_map/finish/pallas_call | solution.py:515

commit v4 on v3

--- a/solution.py
+++ b/solution.py
@@ -200,7 +200,9 @@
             own[l_, m_ // 2, m_ % 2, 15] = tail[96 + lo : 112 + lo]
 
     def owner(i):
-        return (y + 2 + 3 * (i % 4)) % 4, (xh + 1 + i // 4) % 2
+        k = i % 4
+        dy = jnp.where(k == 0, 2, jnp.where(k == 1, 1, jnp.where(k == 2, 3, 0)))
+        return (y + dy) % 4, (xh + 1 + i // 4) % 2
 
     partner = dev(z, x, 1 - core, y)
 
@@ -267,14 +269,38 @@
             remote(b_part(yo, hh, 12), rmb.at[hh], brs.at[1, hh], brr.at[1, hh], y_dev[2]),
         )
 
-    a_sum = (
-        remote(s1b.at[xp % 2, :, xp // 2, pl.ds(0, 4)], fl.at[:, pl.ds(0, 4)], ass.at[0], asr.at[0], x_dev[0]),
-        remote(s1b.at[xm % 2, :, xm // 2, pl.ds(4, 4)], fr.at[:, pl.ds(4, 4)], ass.at[1], asr.at[1], x_dev[2]),
-    )
-    b_sum = (
-        remote(s1b.at[:, yp, :, pl.ds(8, 4)], fd.at[:, :, pl.ds(0, 4)], bss.at[0], bsr.at[0], y_dev[0]),
-        remote(s1b.at[:, ym, :, pl.ds(12, 4)], fu.at[:, :, pl.ds(4, 4)], bss.at[1], bsr.at[1], y_dev[2]),
-    )
+    def a_sum(yy):
+        return (
+            remote(a_part(xp, yy, 0), fl.at[yy, pl.ds(0, 4)], ass.at[0, yy], asr.at[0, yy], x_dev[0]),
+            remote(a_part(xm, yy, 4), fr.at[yy, pl.ds(4, 4)], ass.at[1, yy], asr.at[1, yy], x_dev[2]),
+        )
+
+    def b_sum(hh):
+        return (
+            remote(b_part(yp, hh, 8), fd.at[:, hh, pl.ds(0, 4)], bss.at[0, hh], bsr.at[0, hh], y_dev[0]),
+            remote(b_part(ym, hh, 12), fu.at[:, hh, pl.ds(4, 4)], bss.at[1, hh], bsr.at[1, hh], y_dev[2]),
+        )
+
+    def a_forward(yy):
+        for cp in a_rel(yy):
+            cp.wait_recv()
+        s = own[xp % 2, yy, xp // 2, 0:4] + rpa[yy].astype(F32)
+        s1b[xp % 2, yy, xp // 2, 0:4] = s.astype(BF)
+        s = own[xm % 2, yy, xm // 2, 4:8] + rma[yy].astype(F32)
+        s1b[xm % 2, yy, xm // 2, 4:8] = s.astype(BF)
+        for cp in a_sum(yy):
+            cp.start()
+
+    def b_forward(hh):
+        for cp in b_rel(hh):
+            cp.wait_recv()
+        for l_ in range(2):
+            s = own[l_, yp, hh, 8:12] + rpb[hh, l_].astype(F32)
+            s1b[l_, yp, hh, 8:12] = s.astype(BF)
+            s = own[l_, ym, hh, 12:16] + rmb[hh, l_].astype(F32)
+            s1b[l_, ym, hh, 12:16] = s.astype(BF)
+        for cp in b_sum(hh):
+            cp.start()
 
     def first(i, carry):
         yy, hh = owner(i)
@@ -291,6 +317,9 @@
         pl.when(yy == yo)(lambda: [cp.start() for cp in b_rel(hh)] and None)
         pl.when(yy == yp)(b_dir(hh)[0].start)
         pl.when(yy == ym)(b_dir(hh)[1].start)
+        pl.when(i >= 4)(lambda: a_forward(yy))
+        pl.when(i == 3)(lambda: b_forward((xh + 1) % 2))
+        pl.when(i == 7)(lambda: b_forward(xh))
         return carry
 
     def both(i, carry):
@@ -302,39 +331,15 @@
     lax.fori_loop(LAG, 8, both, 0)
     lax.fori_loop(8 - LAG, 8, first, 0)
     for yy in range(4):
-        for cp in a_rel(yy):
+        for cp in a_dir(yy) + a_sum(yy):
             cp.wait_recv()
-        s = own[xp % 2, yy, xp // 2, 0:4] + rpa[yy].astype(F32)
-        s1b[xp % 2, yy, xp // 2, 0:4] = s.astype(BF)
-        s = own[xm % 2, yy, xm // 2, 4:8] + rma[yy].astype(F32)
-        s1b[xm % 2, yy, xm // 2, 4:8] = s.astype(BF)
-    for cp in a_sum:
-        cp.start()
-    for hh in range(2):
-        for cp in b_rel(hh):
-            cp.wait_recv()
-        for l_ in range(2):
-            s = own[l_, yp, hh, 8:12] + rpb[hh, l_].astype(F32)
-            s1b[l_, yp, hh, 8:12] = s.astype(BF)
-            s = own[l_, ym, hh, 12:16] + rmb[hh, l_].astype(F32)
-            s1b[l_, ym, hh, 12:16] = s.astype(BF)
-    for cp in b_sum:
-        cp.start()
-
-    for yy in range(4):
-        for cp in a_dir(yy):
-            cp.wait_recv()
-    for cp in a_sum:
-        cp.wait_recv()
     for yy in range(4):
         s = own[xl, yy, xh, 0:8] + fl[yy].astype(F32) + fr[yy].astype(F32)
         a1[yy] = s
         a1b[yy] = s.astype(BF)
     for hh in range(2):
-        for cp in b_dir(hh):
+        for cp in b_dir(hh) + b_sum(hh):
             cp.wait_recv()
-    for cp in b_sum:
-        cp.wait_recv()
     for l_ in range(2):
         for hh in range(2):
             s = own[l_, y, hh, 8:16] + fd[l_, hh].astype(F32) + fu[l_, hh].astype(F32)
@@ -342,7 +347,7 @@
             b1b[hh * 2 + l_] = s.astype(BF)
 
     second = []
-    for d in range(3):
+    for d in (1, 0, 2):
         second.append(
             pltpu.make_async_remote_copy(
                 src_ref=a1b.at[(y + d + 1) % 4], dst_ref=ra2.at[d],
@@ -360,11 +365,11 @@
     for cp in second:
         cp.start()
     met(2)
-    sent = list(a_sum) + list(b_sum)
+    sent = []
     for k in range(4):
-        sent += list(a_dir(k)) + list(a_rel(k))
+        sent += a_dir(k) + a_rel(k) + a_sum(k)
     for k in range(2):
-        sent += list(b_dir(k)) + list(b_rel(k))
+        sent += b_dir(k) + b_rel(k) + b_sum(k)
     for cp in sent:
         cp.wait_send()
     for cp in second:
@@ -413,7 +418,7 @@
     fin[...] = total * (1.0 / 512.0)
 
     g_all = []
-    for d in range(7):
+    for d in (2, 4, 3, 0, 6, 1, 5):
         cp = pltpu.make_async_remote_copy(
             src_ref=fin, dst_ref=ag.at[n],
             send_sem=gsnd.at[d], recv_sem=grcv.at[d],
@@ -487,8 +492,8 @@
         dma((4,)),
         dma((8,)), dma((8,)), dma((8,)), dma((8,)),
         dma((8,)), dma((8,)),
-        dma((2, 4)), dma((2, 4)), dma((2, 4)), dma((2, 4)), dma((2,)), dma((2,)),
-        dma((2, 2)), dma((2, 2)), dma((2, 2)), dma((2, 2)), dma((2,)), dma((2,)),
+        dma((2, 4)), dma((2, 4)), dma((2, 4)), dma((2, 4)), dma((2, 4)), dma((2, 4)),
+        dma((2, 2)), dma((2, 2)), dma((2, 2)), dma((2, 2)), dma((2, 2)), dma((2, 2)),
         dma((3,)), dma((3,)), dma((3,)), dma((3,)),
         dma((15,)), dma((15,)),
         dma((7,)), dma((7,)),

time: 53.5 us -> 55.6 us (1.039)
  Pallas kernels: 52.7 us -> 54.8 us
    pallas_call x1, Pallas kernels: 51.8 us -> 53.9 us  [local(): pl.pallas_call(kernel, name='sparse_conv', out_shape=(pltpu.VMEM((8, 8, 8...]
where the time goes in v4:
time: 55.6 us; the launch traced here: 55.4 us
  Pallas kernels  54.8 us (99%)
  between operations  0.64 us (1%)
    pallas_call x1, Pallas kernels, local(): pl.pallas_call(kernel, name='sparse_conv', out_shape=(pltpu.VMEM((8, 8, 8...  53.9 us

profile of v4, /device:TPU:32, one launch (start us, length us, event | category | flops | bytes accessed | tf_op | source)
XLA Modules:
  0.0 55.4 jit_solution(8675583201635317763)
XLA Ops:
  0.6 53.9 %sparse_conv.1 = (bf16[8,8,8,192]{3,2,1,0:T(8,128)(2,1)S(1)}, bf16[8,8,8,192]{3,2,1,0:T(8,128)(2,1)S(1)}, f32[8,16,128]{2,1,0:T(8,128)S(1)}) custom-call(bf16[8,8,8,192]{3,2,1,0:T(8,128)(2,1)} %feat_hbm.1, bf16[192,5184]{1,0:T(8,128)(2,1)} %bitcast.1, s32[8,8,8]{2,1,0:T(8,128)} %mask_hbm.1, bf16[8,8,8,192]{3,2,1,0:T(8,128)(2,1)} %cot_hbm.1), custom_call_target="tpu_custom_call" | custom-call | tf_op jit(solution)/shard_map/sparse_conv/pallas_call | solution.py:505
  54.5 0.9 %finish.1 = (bf16[8,8,8,192]{3,2,1,0:T(8,128)(2,1)}, bf16[8,8,8,192]{3,2,1,0:T(8,128)(2,1)}, f32[3,5184]{1,0:T(4,128)}) custom-call(bf16[8,8,8,192]{3,2,1,0:T(8,128)(2,1)S(1)} %get-tuple-element.6.act_in, bf16[8,8,8,192]{3,2,1,0:T(8,128)(2,1)S(1)} %get-tuple-element.7.gin_in, f32[8,16,128]{2,1,0:T(8,128)S(1)} %get-tuple-element.8.ag_in), custom_call_target="tpu_custom_call" | custom-call | tf_op jit(solution)/shard_map/finish/pallas_call | solution.py:520

commit v5 on v4

--- a/solution.py
+++ b/solution.py
@@ -185,7 +185,6 @@
         gp2[rows, :] = g.astype(BF)
         ghalo[1 + xx, 1:9] = g.reshape(8, 8, C).astype(BF)
 
-    g_copies = exchange(ghalo, gsend, grecv)
 
     gpt[...] = lax.dot_general(
         permv[...], gp2[...], (((1,), (1,)), ((), ())), preferred_element_type=F32
@@ -364,6 +363,7 @@
         )
     for cp in second:
         cp.start()
+    g_copies = exchange(ghalo, gsend, grecv)
     met(2)
     sent = []
     for k in range(4):

time: 55.6 us -> 55.8 us (level)
  no operation moved by 1% of the time
where the time goes in v5:
time: 55.8 us; the launch traced here: 55.6 us
  Pallas kernels  55 us (99%)
  between operations  0.64 us (1%)
    pallas_call x1, Pallas kernels, local(): pl.pallas_call(kernel, name='sparse_conv', out_shape=(pltpu.VMEM((8, 8, 8...  54.1 us

profile of v5, /device:TPU:32, one launch (start us, length us, event | category | flops | bytes accessed | tf_op | source)
XLA Modules:
  0.0 55.6 jit_solution(1456131934771030880)
XLA Ops:
  0.6 54.1 %sparse_conv.1 = (bf16[8,8,8,192]{3,2,1,0:T(8,128)(2,1)S(1)}, bf16[8,8,8,192]{3,2,1,0:T(8,128)(2,1)S(1)}, f32[8,16,128]{2,1,0:T(8,128)S(1)}) custom-call(bf16[8,8,8,192]{3,2,1,0:T(8,128)(2,1)} %feat_hbm.1, bf16[192,5184]{1,0:T(8,128)(2,1)} %bitcast.1, s32[8,8,8]{2,1,0:T(8,128)} %mask_hbm.1, bf16[8,8,8,192]{3,2,1,0:T(8,128)(2,1)} %cot_hbm.1), custom_call_target="tpu_custom_call" | custom-call | tf_op jit(solution)/shard_map/sparse_conv/pallas_call | solution.py:505
  54.7 0.9 %finish.1 = (bf16[8,8,8,192]{3,2,1,0:T(8,128)(2,1)}, bf16[8,8,8,192]{3,2,1,0:T(8,128)(2,1)}, f32[3,5184]{1,0:T(4,128)}) custom-call(bf16[8,8,8,192]{3,2,1,0:T(8,128)(2,1)S(1)} %get-tuple-element.6.act_in, bf16[8,8,8,192]{3,2,1,0:T(8,128)(2,1)S(1)} %get-tuple-element.7.gin_in, f32[8,16,128]{2,1,0:T(8,128)S(1)} %get-tuple-element.8.ag_in), custom_call_target="tpu_custom_call" | custom-call | tf_op jit(solution)/shard_map/finish/pallas_call | solution.py:520

commit v6 on v2

--- a/solution.py
+++ b/solution.py
@@ -57,7 +57,7 @@
     act_ref, gin_ref, ag,
     wv, mask, cot, halo, ghalo, even, odd, cols, pre, live, gp2, gpt,
     own, sb, rb, s1b, a1, b1, a1b, b1b, tb, zb, fin,
-    ra, rby, ra2, rb2, rz,
+    ra, rby, ra2, rb2, rz, permv, turnv,
     lsem, hsend, hrecv, gsend, grecv, csend, crecv,
     asend, arecv, bsend, brecv, a2send, a2recv, b2send, b2recv,
     zsend, zrecv, gsnd, grcv, ring,
@@ -75,7 +75,7 @@
         return {"wide": (z_ * 2 + x_ % 2) * 2 + c_, "narrow": y_ * 2 + x_ // 2}
 
     near = []
-    for dw, dn in ((1, 0), (-1, 0), (0, 1), (0, -1), (1, 1), (1, -1), (-1, 1), (-1, -1)):
+    for dw, dn in ((1, 1), (1, -1), (-1, 1), (-1, -1), (0, 1), (0, -1), (1, 0), (-1, 0)):
         near.append(
             (dw, dn, {"wide": (w + dw + WIDE) % WIDE, "narrow": (n + dn + NARROW) % NARROW})
         )
@@ -142,6 +142,19 @@
 
     halo_copies = exchange(halo, hsend, hrecv)
     cols[:, 5120:5248] = jnp.zeros((512, 128), BF)
+    r = iota((C, C), 0)
+    q = (r >= 96).astype(jnp.int32)
+    r = r - 96 * q
+    rl = (r >= 48).astype(jnp.int32)
+    r = r - 48 * rl
+    rk = (r >= 16).astype(jnp.int32) + (r >= 32).astype(jnp.int32)
+    rz_ = r - 16 * rk
+    rc = jnp.where(q == 1, core, 1 - core)
+    rj = 3 * ((rz_ * 2 + rl) * 2 + rc) + rk
+    permv[...] = (rj == iota((C, C), 1)).astype(F32).astype(BF)
+    rr = iota((256, 256), 0)
+    turnv[...] = (iota((256, 256), 1) == (rr % 16) * 16 + rr // 16).astype(F32).astype(BF)
+
     for cp in halo_copies:
         cp.wait()
     met(0)
@@ -174,18 +187,8 @@
 
     g_copies = exchange(ghalo, gsend, grecv)
 
-    r = iota((C, C), 0)
-    q = (r >= 96).astype(jnp.int32)
-    r = r - 96 * q
-    rl = (r >= 48).astype(jnp.int32)
-    r = r - 48 * rl
-    rk = (r >= 16).astype(jnp.int32) + (r >= 32).astype(jnp.int32)
-    rz_ = r - 16 * rk
-    rc = jnp.where(q == 1, core, 1 - core)
-    rj = 3 * ((rz_ * 2 + rl) * 2 + rc) + rk
-    perm = (rj == iota((C, C), 1)).astype(F32).astype(BF)
     gpt[...] = lax.dot_general(
-        perm, gp2[...], (((1,), (1,)), ((), ())), preferred_element_type=F32
+        permv[...], gp2[...], (((1,), (1,)), ((), ())), preferred_element_type=F32
     ).astype(BF)
 
     tail = jnp.dot(gpt[...], cols[:, 5120:5248], preferred_element_type=F32)
@@ -309,7 +312,7 @@
             b1b[hh * 2 + l_] = s.astype(BF)
 
     second = []
-    for d in range(3):
+    for d in (1, 0, 2):
         second.append(
             pltpu.make_async_remote_copy(
                 src_ref=a1b.at[(y + d + 1) % 4], dst_ref=ra2.at[d],
@@ -338,10 +341,8 @@
     tb[0:128] = sa.reshape(128, 128).astype(BF)
     tb[128:256] = sbb.reshape(128, 128).astype(BF)
 
-    rr = iota((256, 256), 0)
-    turn = (iota((256, 256), 1) == (rr % 16) * 16 + rr // 16).astype(F32).astype(BF)
     zb[...] = (
-        jnp.dot(turn, tb[...], preferred_element_type=F32).astype(BF).reshape(16, 16, 128)
+        jnp.dot(turnv[...], tb[...], preferred_element_type=F32).astype(BF).reshape(16, 16, 128)
     )
     z_copies = []
     for d in range(15):
@@ -376,7 +377,7 @@
     fin[...] = total * (1.0 / 512.0)
 
     g_all = []
-    for d in range(7):
+    for d in (2, 4, 3, 0, 6, 1, 5):
         cp = pltpu.make_async_remote_copy(
             src_ref=fin, dst_ref=ag.at[n],
             send_sem=gsnd.at[d], recv_sem=grcv.at[d],
@@ -444,6 +445,7 @@
         vmem((3, 8, 16, 128), BF),
         vmem((3, 8, 16, 128), BF),
         vmem((15, 16, 128), BF),
+        vmem((C, C), BF), vmem((256, 256), BF),
         dma((4,)),
         dma((8,)), dma((8,)), dma((8,)), dma((8,)),
         dma((8,)), dma((8,)),

time: 53.1 us -> 52.4 us (0.987)
  Pallas kernels: 52.3 us -> 51.7 us
    pallas_call x1, Pallas kernels: 51.4 us -> 50.7 us  [local(): pl.pallas_call(kernel, name='sparse_conv', out_shape=(pltpu.VMEM((8, 8, 8...]
where the time goes in v6:
time: 52.4 us; the launch traced here: 52.3 us
  Pallas kernels  51.7 us (99%)
  between operations  0.64 us (1%)
    pallas_call x1, Pallas kernels, local(): pl.pallas_call(kernel, name='sparse_conv', out_shape=(pltpu.VMEM((8, 8, 8...  50.7 us

profile of v6, /device:TPU:8, one launch (start us, length us, event | category | flops | bytes accessed | tf_op | source)
XLA Modules:
  0.0 52.3 jit_solution(15108193606723097064)
XLA Ops:
  0.6 50.7 %sparse_conv.1 = (bf16[8,8,8,192]{3,2,1,0:T(8,128)(2,1)S(1)}, bf16[8,8,8,192]{3,2,1,0:T(8,128)(2,1)S(1)}, f32[8,16,128]{2,1,0:T(8,128)S(1)}) custom-call(bf16[8,8,8,192]{3,2,1,0:T(8,128)(2,1)} %feat_hbm.1, bf16[192,5184]{1,0:T(8,128)(2,1)} %bitcast.1, s32[8,8,8]{2,1,0:T(8,128)} %mask_hbm.1, bf16[8,8,8,192]{3,2,1,0:T(8,128)(2,1)} %cot_hbm.1), custom_call_target="tpu_custom_call" | custom-call | tf_op jit(solution)/shard_map/sparse_conv/pallas_call | solution.py:462
  51.4 0.9 %finish.1 = (bf16[8,8,8,192]{3,2,1,0:T(8,128)(2,1)}, bf16[8,8,8,192]{3,2,1,0:T(8,128)(2,1)}, f32[3,5184]{1,0:T(4,128)}) custom-call(bf16[8,8,8,192]{3,2,1,0:T(8,128)(2,1)S(1)} %get-tuple-element.6.act_in, bf16[8,8,8,192]{3,2,1,0:T(8,128)(2,1)S(1)} %get-tuple-element.7.gin_in, f32[8,16,128]{2,1,0:T(8,128)S(1)} %get-tuple-element.8.ag_in), custom_call_target="tpu_custom_call" | custom-call | tf_op jit(solution)/shard_map/finish/pallas_call | solution.py:477

commit v7 on v6

--- a/solution.py
+++ b/solution.py
@@ -10,7 +10,7 @@
 F32 = jnp.float32
 MESH = pl.DeviceIdType.MESH
 WIDE, NARROW = 64, 8
-LAG = 3
+LAG = 2
 
 
 def iota(shape, dim):
@@ -85,7 +85,7 @@
     n_dev = [{"wide": w, "narrow": (n + d) % 8} for d in range(1, 8)]
 
     barrier = pltpu.get_barrier_semaphore()
-    partners = [t[2] for t in near] + n_dev + x_dev + [z_dev[0], z_dev[14]]
+    partners = [t[2] for t in near] + n_dev[1:6] + x_dev + [z_dev[0], z_dev[14]]
     for p in partners:
         pl.semaphore_signal(barrier, inc=1, device_id=p, device_id_type=MESH)
 

time: 52.4 us -> 52.5 us (level)
  no operation moved by 1% of the time
where the time goes in v7:
time: 52.5 us; the launch traced here: 52.3 us
  Pallas kernels  51.7 us (98%)
  between operations  0.64 us (1%)
    pallas_call x1, Pallas kernels, local(): pl.pallas_call(kernel, name='sparse_conv', out_shape=(pltpu.VMEM((8, 8, 8...  50.8 us

profile of v7, /device:TPU:8, one launch (start us, length us, event | category | flops | bytes accessed | tf_op | source)
XLA Modules:
  0.0 52.3 jit_solution(11201719079867805380)
XLA Ops:
  0.6 50.8 %sparse_conv.1 = (bf16[8,8,8,192]{3,2,1,0:T(8,128)(2,1)S(1)}, bf16[8,8,8,192]{3,2,1,0:T(8,128)(2,1)S(1)}, f32[8,16,128]{2,1,0:T(8,128)S(1)}) custom-call(bf16[8,8,8,192]{3,2,1,0:T(8,128)(2,1)} %feat_hbm.1, bf16[192,5184]{1,0:T(8,128)(2,1)} %bitcast.1, s32[8,8,8]{2,1,0:T(8,128)} %mask_hbm.1, bf16[8,8,8,192]{3,2,1,0:T(8,128)(2,1)} %cot_hbm.1), custom_call_target="tpu_custom_call" | custom-call | tf_op jit(solution)/shard_map/sparse_conv/pallas_call | solution.py:462
  51.4 0.9 %finish.1 = (bf16[8,8,8,192]{3,2,1,0:T(8,128)(2,1)}, bf16[8,8,8,192]{3,2,1,0:T(8,128)(2,1)}, f32[3,5184]{1,0:T(4,128)}) custom-call(bf16[8,8,8,192]{3,2,1,0:T(8,128)(2,1)S(1)} %get-tuple-element.6.act_in, bf16[8,8,8,192]{3,2,1,0:T(8,128)(2,1)S(1)} %get-tuple-element.7.gin_in, f32[8,16,128]{2,1,0:T(8,128)S(1)} %get-tuple-element.8.ag_in), custom_call_target="tpu_custom_call" | custom-call | tf_op jit(solution)/shard_map/finish/pallas_call | solution.py:477
